TPU v7x, 256 devices: a whole 4x4x8 slice. The times are simulated.
256 devices in a mesh: expert: 64 (over y, z, core), etp: 4 (over x).
Axes of the slice: x: 4, y: 4, z: 8, core: 2. Of those that a mesh axis runs over, the one named last changes fastest.
Arguments:
- tokens: bfloat16 [8192, 2048], P('expert'), may hold values from -6 to 6
- grad_out: bfloat16 [8192, 2048], P('expert'), may hold values from -6 to 6
- routes: int32 [8192, 8], P('expert'), may hold values from 0 to 127, all different within a row; in each aligned block of 128 rows (0 to 127, 128 to 255, ...) at most 10 rows name the same one
- probs: bfloat16 [8192, 8], P('expert'), may hold values from 0.049804688 to 0.3984375
- w_gate: bfloat16 [128, 768, 2048], P('expert', 'etp'), may hold values from -0.125 to 0.125
- w_up: bfloat16 [128, 768, 2048], P('expert', 'etp'), may hold values from -0.125 to 0.125
- w_down: bfloat16 [128, 768, 2048], P('expert', 'etp'), may hold values from -0.21875 to 0.21875
Outputs:
- grad_tokens: bfloat16 [8192, 2048], P('expert')
- grad_probs: bfloat16 [8192, 8], P('expert')
- grad_gate: bfloat16 [128, 768, 2048], P('expert', 'etp')
- grad_up: bfloat16 [128, 768, 2048], P('expert', 'etp')
- grad_down: bfloat16 [128, 768, 2048], P('expert', 'etp')
Inputs may be any that keep to these rules, and one draw needn't show every extreme that they name: `routes`: each row names 8 different experts. Among the 128 rows of one device no expert is named by more than 10 rows, a bound that some block reaches.
All inputs are finite; a program needn't handle non-finite values.
Results may differ from a plain program's by a relative error of at most 0.018.
Values may be sent and summed in bfloat16 or wider, within the bound.
A program may use at most 128 MiB of HBM per device.

v0:
```python
import jax
import jax.numpy as jnp
from jax import lax
from jax.sharding import PartitionSpec as P


def token_sum(slot_rows, target, tok_rows, top_count):
    columns = slot_rows.shape[-1]
    picked = slot_rows.reshape(-1, columns)[target]
    return jnp.sum(picked.reshape(tok_rows, top_count, columns).astype(jnp.float32), axis=1).astype(
        jnp.bfloat16
    )


def expert_major(values, sources, local_experts, capacity):
    tail = values.shape[2:]
    shaped = values.reshape((sources, local_experts, capacity) + tail)
    order = (1, 0, 2) + tuple(range(3, 3 + len(tail)))
    return jnp.transpose(shaped, order).reshape((local_experts, sources * capacity) + tail)


def source_major(values, sources, local_experts, capacity):
    tail = values.shape[2:]
    shaped = values.reshape((local_experts, sources, capacity) + tail)
    order = (1, 0, 2) + tuple(range(3, 3 + len(tail)))
    return jnp.transpose(shaped, order).reshape((sources, local_experts * capacity) + tail)


def body(tokens, grad_out, routes, probs, w_gate, w_up, w_down):
    sources = lax.axis_size("expert")
    local_experts = w_gate.shape[0]
    hid_units = w_gate.shape[1]
    expert_count = sources * local_experts
    tok_rows, top_count = routes.shape
    model_width = tokens.shape[1]
    capacity = max(2, 5 * tok_rows * top_count // (4 * expert_count))
    pair_count = tok_rows * top_count
    flat_routes = routes.reshape(-1)
    one_hot = (flat_routes[:, None] == jnp.arange(expert_count, dtype=jnp.int32)[None, :]).astype(
        jnp.int32
    )
    slot_rank = jnp.sum(jnp.cumsum(one_hot, axis=0) * one_hot, axis=1) - 1
    target = flat_routes * capacity + slot_rank
    slot_table = (
        jnp.full((expert_count * capacity,), pair_count, jnp.int32)
        .at[target]
        .set(jnp.arange(pair_count, dtype=jnp.int32))
    )
    filled = slot_table < pair_count
    safe_index = jnp.where(filled, slot_table, 0)
    token_of = safe_index // top_count
    block_rows = local_experts * capacity
    send_prob = jnp.where(filled, probs.reshape(-1)[safe_index], 0).reshape(sources, block_rows)
    send_rows = jnp.where(filled[:, None], tokens[token_of], 0).reshape(
        sources, block_rows, model_width
    )
    send_grad = jnp.where(filled[:, None], grad_out[token_of], 0).reshape(
        sources, block_rows, model_width
    )
    recv_rows, recv_grad, recv_prob = (
        lax.all_to_all(send_rows, "expert", split_axis=0, concat_axis=0, tiled=True),
        lax.all_to_all(send_grad, "expert", split_axis=0, concat_axis=0, tiled=True),
        lax.all_to_all(send_prob, "expert", split_axis=0, concat_axis=0, tiled=True),
    )
    in_rows = expert_major(recv_rows, sources, local_experts, capacity)
    in_grad = expert_major(recv_grad, sources, local_experts, capacity)
    weight = expert_major(recv_prob, sources, local_experts, capacity).astype(jnp.float32)[
        ..., None
    ]
    gate_up = jnp.concatenate([w_gate, w_up], axis=1)
    both_pre = jnp.einsum("end,ehd->enh", in_rows, gate_up, preferred_element_type=jnp.float32)
    pre_gate = both_pre[..., :hid_units]
    pre_up = both_pre[..., hid_units:]
    back_grad = jnp.einsum("end,ehd->enh", in_grad, w_down, preferred_element_type=jnp.float32)
    sigma_gate = jax.nn.sigmoid(pre_gate)
    activated = pre_gate * sigma_gate
    hidden = (activated * pre_up).astype(jnp.bfloat16)
    prob_local = jnp.sum(hidden.astype(jnp.float32) * back_grad, axis=-1)
    prob_part = source_major(prob_local, sources, local_experts, capacity)
    scaled = (weight * in_grad.astype(jnp.float32)).astype(jnp.bfloat16)
    grad_down = jnp.einsum(
        "enh,end->ehd", hidden, scaled, preferred_element_type=jnp.float32
    ).astype(jnp.bfloat16)
    hidden_grad = weight * back_grad
    d_gate = (hidden_grad * pre_up * sigma_gate * (1.0 + pre_gate * (1.0 - sigma_gate))).astype(
        jnp.bfloat16
    )
    d_up = (hidden_grad * activated).astype(jnp.bfloat16)
    d_both = jnp.concatenate([d_gate, d_up], axis=-1)
    grad_both = jnp.einsum(
        "enh,end->ehd", d_both, in_rows, preferred_element_type=jnp.float32
    ).astype(jnp.bfloat16)
    grad_gate = grad_both[:, :hid_units]
    grad_up = grad_both[:, hid_units:]
    local_part = jnp.einsum(
        "enh,ehd->end", d_both, gate_up, preferred_element_type=jnp.float32
    ).astype(jnp.bfloat16)
    partial_sum = source_major(local_part, sources, local_experts, capacity).astype(jnp.float32)
    totals, prob_total = (
        lax.psum(partial_sum.astype(jnp.bfloat16), "etp").astype(jnp.float32),
        lax.psum(prob_part.astype(jnp.bfloat16), "etp").astype(jnp.float32),
    )
    back_rows, back_prob = (
        lax.all_to_all(
            totals.astype(jnp.bfloat16), "expert", split_axis=0, concat_axis=0, tiled=True
        ),
        lax.all_to_all(
            prob_total.astype(jnp.bfloat16), "expert", split_axis=0, concat_axis=0, tiled=True
        ),
    )
    grad_tokens = token_sum(back_rows, target, tok_rows, top_count)
    grad_probs = back_prob.reshape(-1)[target].reshape(tok_rows, top_count)
    return (grad_tokens, grad_probs, grad_gate, grad_up, grad_down)


def solution(mesh):
    return jax.shard_map(
        body,
        mesh=mesh,
        in_specs=(
            P("expert", None),
            P("expert", None),
            P("expert", None),
            P("expert", None),
            P("expert", "etp", None),
            P("expert", "etp", None),
            P("expert", "etp", None),
        ),
        out_specs=(
            P("expert", None),
            P("expert", None),
            P("expert", "etp", None),
            P("expert", "etp", None),
            P("expert", "etp", None),
        ),
        check_vma=False,
    )
```

profile of v0, /device:TPU:1, one launch (start us, length us, event | category | flops | bytes accessed | tf_op | source)
XLA Modules:
  0.0 739.5 jit_solution(8986756804399492162)
XLA Ops:
  15.4 8.0 %gather_fusion = bf16[1280]{0:T(1024)(128)(2,1)S(1)} fusion(bf16[1024]{0:T(1024)(128)(2,1)S(1)} %reshape.132, s32[2048]{0:T(1024)S(1)} %pad_clamp_fusion.1), kind=kCustom, calls=%fused_computation | custom fusion | bytes 10240 | tf_op jit(solution)/shard_map/gather | solution.py:53
  24.1 13.2 %all-to-all-start = ((bf16[64,1,20]{2,1,0:T(2,128)(2,1)}), bf16[64,1,20]{2,1,0:T(2,128)(2,1)S(1)}, u32[]{:S(2)}, u32[]{:S(2)}) async-start(bf16[64,1,20]{2,1,0:T(2,128)(2,1)} %all_to_all.28), calls=%async_computation | async-start | bytes 65536 | tf_op jit(solution)/shard_map/all_to_all | solution.py:63
  43.6 9.0 %gather.23 = bf16[64,20,2048]{2,1,0:T(8,128)(2,1)} reshape(bf16[1280,2048]{1,0:T(8,128)(2,1)} %gather_fusion.2) | data formatting | bytes 10485760 | tf_op jit(solution)/shard_map/gather | solution.py:54
  58.8 8.9 %gather.21 = bf16[64,20,2048]{2,1,0:T(8,128)(2,1)} reshape(bf16[1280,2048]{1,0:T(8,128)(2,1)} %gather_fusion.1) | data formatting | bytes 10485760 | tf_op jit(solution)/shard_map/gather | solution.py:57
  67.8 10.2 %broadcast_select_fusion = (bf16[64,20,2048]{2,1,0:T(8,128)(2,1)}, bf16[64,20,2048]{2,1,0:T(8,128)(2,1)}) fusion(bf16[64,20,2048]{2,1,0:T(8,128)(2,1)} %gather.23, pred[64,20]{1,0:T(8,128)(4,1)S(1)} %broadcast_in_dim.43, bf16[64,20,2048]{2,1,0:T(8,128)(2,1)} %gather.21), kind=kLoop, calls=%fused_computation.7 | loop fusion | flops 5242880 | bytes 20972800 | tf_op jit(solution)/shard_map/jit(_where)/select_n | solution.py:54
  78.0 151.6 %all_to_all.34 = bf16[64,20,2048]{2,1,0:T(8,128)(2,1)} all-to-all(bf16[64,20,2048]{2,1,0:T(8,128)(2,1)} %get-tuple-element.30), channel_id=1, replica_groups=mesh['expert'=64,'etp'=4] {'expert'}, dimensions={0} | all-to-all | bytes 10485760 | tf_op jit(solution)/shard_map/all_to_all | solution.py:61
  240.3 8.0 %copy.74 = bf16[64,20,2048]{2,0,1:T(8,128)(2,1)} copy(bf16[64,20,2048]{2,1,0:T(8,128)(2,1)} %all_to_all.34) | data formatting | bytes 10485760 | tf_op jit(solution)/shard_map/all_to_all | solution.py:61
  248.3 10.3 %copy.75 = bf16[2,64,10,2048]{3,0,2,1:T(2,128)(2,1)} copy(bf16[2,64,10,2048]{3,1,2,0:T(8,128)(2,1)} %bitcast.38) | data formatting | bytes 10485760 | tf_op jit(solution)/shard_map/transpose | solution.py:19
  258.6 118.0 %all-to-all-done.1 = bf16[64,20,2048]{2,1,0:T(8,128)(2,1)} async-done(((bf16[64,20,2048]{2,1,0:T(8,128)(2,1)}), bf16[64,20,2048]{2,1,0:T(8,128)(2,1)}, u32[]{:S(2)}, u32[]{:S(2)}) %all-to-all-start.1) | async-done | bytes 5242912 | tf_op jit(solution)/shard_map/all_to_all | solution.py:62
  376.5 8.5 %copy.71 = bf16[64,20,2048]{2,0,1:T(8,128)(2,1)} copy(bf16[64,20,2048]{2,1,0:T(8,128)(2,1)} %all-to-all-done.1) | data formatting | bytes 10485760 | tf_op jit(solution)/shard_map/all_to_all | solution.py:62
  385.0 10.2 %copy.72 = bf16[2,64,10,2048]{3,0,2,1:T(2,128)(2,1)} copy(bf16[2,64,10,2048]{3,1,2,0:T(8,128)(2,1)} %bitcast.39) | data formatting | bytes 10485760 | tf_op jit(solution)/shard_map/transpose | solution.py:19
  395.2 7.4 fusion.6
  408.5 7.1 convolution_convert_fusion
  415.6 10.2 %copy.78 = bf16[2,640,2048]{2,0,1:T(2,128)(2,1)} copy(bf16[2,640,2048]{2,1,0:T(8,128)(2,1)} %convolution_convert_fusion) | data formatting | bytes 10485760 | tf_op jit(solution)/shard_map/convert_element_type | solution.py:97
  425.8 7.9 %copy.79 = bf16[64,2,10,2048]{3,0,2,1:T(8,128)(2,1)} copy(bf16[64,2,10,2048]{3,1,2,0:T(2,128)(2,1)} %bitcast.40) | data formatting | bytes 10485760 | tf_op jit(solution)/shard_map/transpose | solution.py:26
  434.0 8.6 %psum.15 = bf16[64,1,20]{0,2,1:T(8,128)(2,1)S(1)} all-reduce(bf16[64,1,20]{0,2,1:T(8,128)(2,1)S(1)} %all_to_all.26), channel_id=1, replica_groups=mesh['expert'=64,'etp'=4] {'etp'}, use_global_device_ids=true, to_apply=%region_7.8 | all-reduce | flops 1280 | bytes 5120 | tf_op jit(solution)/shard_map/psum | solution.py:101
  443.3 7.7 %all-to-all-start.4 = ((bf16[64,1,20]{2,1,0:T(2,128)(2,1)}), bf16[64,1,20]{2,1,0:T(2,128)(2,1)S(1)}, u32[]{:S(2)}, u32[]{:S(2)}) async-start(bf16[64,1,20]{2,1,0:T(2,128)(2,1)} %copy.82), calls=%async_computation.4 | async-start | bytes 65536 | tf_op jit(solution)/shard_map/all_to_all | solution.py:107
  451.0 94.3 %all-reduce.2.cloned.1.call-done = bf16[64,20,2048]{2,0,1:T(8,128)(2,1)} async-done(((bf16[64,20,2048]{2,0,1:T(8,128)(2,1)}), bf16[64,20,2048]{2,0,1:T(8,128)(2,1)}) %all-reduce.2.cloned.1.call-update) | async-done | bytes 5242896 | tf_op jit(solution)/shard_map/psum | solution.py:100
  545.3 8.1 %copy.80 = bf16[64,20,2048]{2,1,0:T(8,128)(2,1)} copy(bf16[64,20,2048]{2,0,1:T(8,128)(2,1)} %all-reduce.2.cloned.1.call-done) | data formatting | bytes 10485760 | tf_op jit(solution)/shard_map/psum | solution.py:100
  553.4 11.0 %all-to-all-start.3 = ((bf16[64,20,2048]{2,1,0:T(8,128)(2,1)}), bf16[64,20,2048]{2,1,0:T(8,128)(2,1)}, u32[]{:S(2)}, u32[]{:S(2)}) async-start(bf16[64,20,2048]{2,1,0:T(8,128)(2,1)} %copy.80), calls=%async_computation.3 | async-start | bytes 12582912 | tf_op jit(solution)/shard_map/all_to_all | solution.py:104
  582.0 6.8 gather_fusion.4
  589.5 115.7 %all-to-all-done.3 = bf16[64,20,2048]{2,1,0:T(8,128)(2,1)} async-done(((bf16[64,20,2048]{2,1,0:T(8,128)(2,1)}), bf16[64,20,2048]{2,1,0:T(8,128)(2,1)}, u32[]{:S(2)}, u32[]{:S(2)}) %all-to-all-start.3) | async-done | bytes 5242912 | tf_op jit(solution)/shard_map/all_to_all | solution.py:104
  705.3 9.0 %reshape.139 = bf16[1280,2048]{1,0:T(8,128)(2,1)} reshape(bf16[64,20,2048]{2,1,0:T(8,128)(2,1)} %all-to-all-done.3) | data formatting | bytes 10485760 | tf_op jit(solution)/shard_map/reshape | solution.py:9
  714.3 12.1 %gather_fusion.3 = bf16[1024,2048]{1,0:T(8,128)(2,1)} fusion(bf16[1280,2048]{1,0:T(8,128)(2,1)} %reshape.139, s32[1024]{0:T(1024)S(1)} %broadcast_clamp_fusion), kind=kCustom, calls=%fused_computation.3 | custom fusion | bytes 8392704 | tf_op jit(solution)/shard_map/gather | solution.py:9
  (80 shorter events, 63.1 us)
Async XLA Ops:
  7.2 395.4 %copy-start = (bf16[2,192,2048]{2,1,0:T(8,128)(2,1)S(1)}, bf16[2,192,2048]{2,1,0:T(8,128)(2,1)}, u32[]{:S(2)}) copy-start(bf16[2,192,2048]{2,1,0:T(8,128)(2,1)} %param.13) | copy-start | bytes 4718596
  7.2 30.2 %copy-start.2 = (bf16[128,2048]{1,0:T(8,128)(2,1)S(1)}, bf16[128,2048]{1,0:T(8,128)(2,1)}, u32[]{:S(2)}) copy-start(bf16[128,2048]{1,0:T(8,128)(2,1)} %param.7) | copy-start | bytes 1572868
  24.1 53.9 %all-to-all-start = ((bf16[64,1,20]{2,1,0:T(2,128)(2,1)}), bf16[64,1,20]{2,1,0:T(2,128)(2,1)S(1)}, u32[]{:S(2)}, u32[]{:S(2)}) async-start(bf16[64,1,20]{2,1,0:T(2,128)(2,1)} %all_to_all.28), calls=%async_computation | async-start | bytes 65536 | tf_op jit(solution)/shard_map/all_to_all | solution.py:63
  43.6 9.0 %copy-start.3 = (bf16[128,2048]{1,0:T(8,128)(2,1)S(1)}, bf16[128,2048]{1,0:T(8,128)(2,1)}, u32[]{:S(2)}) copy-start(bf16[128,2048]{1,0:T(8,128)(2,1)} %param.8) | copy-start | bytes 1572868
  229.5 6.4 copy-start.5
  229.5 147.0 %all-to-all-start.1 = ((bf16[64,20,2048]{2,1,0:T(8,128)(2,1)}), bf16[64,20,2048]{2,1,0:T(8,128)(2,1)}, u32[]{:S(2)}, u32[]{:S(2)}) async-start(bf16[64,20,2048]{2,1,0:T(8,128)(2,1)} %get-tuple-element.31), calls=%async_computation.1 | async-start | bytes 12582912 | tf_op jit(solution)/shard_map/all_to_all | solution.py:62
  235.7 309.6 %all-reduce.2.cloned.1.call-start = ((), (), s32[]{:S(2)}) async-start(), calls=%async_computation.5 | async-start | bytes 10485760 | tf_op jit(solution)/shard_map/psum | solution.py:100
  395.2 7.4 %copy-start.4 = (bf16[2,64,10,2048]{3,0,2,1:T(2,128)(2,1)S(1)}, bf16[2,64,10,2048]{3,0,2,1:T(2,128)(2,1)}, u32[]{:S(2)}) copy-start(bf16[2,64,10,2048]{3,0,2,1:T(2,128)(2,1)} %copy.72) | copy-start | bytes 15728644
  407.7 0.8 copy-start.6
  443.3 110.1 %all-to-all-start.4 = ((bf16[64,1,20]{2,1,0:T(2,128)(2,1)}), bf16[64,1,20]{2,1,0:T(2,128)(2,1)S(1)}, u32[]{:S(2)}, u32[]{:S(2)}) async-start(bf16[64,1,20]{2,1,0:T(2,128)(2,1)} %copy.82), calls=%async_computation.4 | async-start | bytes 65536 | tf_op jit(solution)/shard_map/all_to_all | solution.py:107
  553.4 22.1 %slice-start = ((s8[5242880]{0:T(1024)(128)(4,1)}), s8[1048576]{0:T(1024)(128)(4,1)S(1)}, s32[]{:S(2)}) async-start(s8[5242880]{0:T(1024)(128)(4,1)} %bitcast.42), calls=%async_computation.6 | async-start | bytes 2097152
  553.4 151.9 %all-to-all-start.3 = ((bf16[64,20,2048]{2,1,0:T(8,128)(2,1)}), bf16[64,20,2048]{2,1,0:T(8,128)(2,1)}, u32[]{:S(2)}, u32[]{:S(2)}) async-start(bf16[64,20,2048]{2,1,0:T(8,128)(2,1)} %copy.80), calls=%async_computation.3 | async-start | bytes 12582912 | tf_op jit(solution)/shard_map/all_to_all | solution.py:104
  564.6 6.2 copy-start.8
  564.6 10.8 %slice-start.1 = ((s8[5242880]{0:T(1024)(128)(4,1)}), s8[4194304]{0:T(1024)(128)(4,1)S(1)}, s32[]{:S(2)}) async-start(s8[5242880]{0:T(1024)(128)(4,1)} %bitcast.42), calls=%async_computation.7 | async-start | bytes 8388608
  570.8 4.7 copy-start.7
  714.3 18.0 %copy-start.1 = (bf16[2,192,2048]{2,1,0:T(8,128)(2,1)S(1)}, bf16[2,192,2048]{2,1,0:T(8,128)(2,1)}, u32[]{:S(2)}) copy-start(bf16[2,192,2048]{2,1,0:T(8,128)(2,1)} %param.13) | copy-start | bytes 4718596
Sparse Core Ops, SparseCore 0:
  433.8 111.4 all-reduce.1
where the time goes:
time: 747 us; the launch traced here: 739 us
  waiting for transfers between devices  328 us (44%)
  blocking collectives  160 us (21%)
  local copies, waits for them, and re-layouts  146 us (20%)
  starting transfers between devices  38.3 us (5%)
  matrix products  28.6 us (4%)
  other arithmetic  23.9 us (3%)
  between operations  14.7 us (2%)
    all_to_all x1, blocking collectives, body(): lax.all_to_all(send_rows, 'expert', split_axis=0, concat_axis=0, tiled=True)  152 us
    all_to_all x1, waiting for transfers between devices, body(): lax.all_to_all(send_grad, 'expert', split_axis=0, concat_axis=0, tiled=True)  118 us
    all_to_all x1, waiting for transfers between devices, body(): lax.all_to_all(totals.astype(jnp.bfloat16), 'expert', split_axis=0, conca...  116 us
    psum x1, waiting for transfers between devices, body(): lax.psum(partial_sum.astype(jnp.bfloat16), 'etp').astype(jnp.float32)  94.3 us
    transpose x2, local copies, waits for them, and re-layouts, expert_major(): jnp.transpose(shaped, order)  20.5 us
    gather x2, local copies, waits for them, and re-layouts, body(): tokens[token_of]  15.2 us
    gather x2, local copies, waits for them, and re-layouts, body(): grad_out[token_of]  15.1 us
  transfers between devices with their start and end apart: 5, of which 3 were waited for; matrix products, arithmetic and copies ran while one was open for 13% of the time, Pallas kernels for 0%

commit v1 on v0

--- a/solution.py
+++ b/solution.py
@@ -97,7 +97,9 @@
     ).astype(jnp.bfloat16)
     partial_sum = source_major(local_part, sources, local_experts, capacity).astype(jnp.float32)
     totals, prob_total = (
-        lax.psum(partial_sum.astype(jnp.bfloat16), "etp").astype(jnp.float32),
+        jnp.sum(lax.all_gather(partial_sum.astype(jnp.bfloat16), "etp"), axis=0).astype(
+            jnp.float32
+        ),
         lax.psum(prob_part.astype(jnp.bfloat16), "etp").astype(jnp.float32),
     )
     back_rows, back_prob = (

time: 747 us -> 839 us (1.12)
  waiting for transfers between devices: 328 us -> 405 us
  other arithmetic: 23.9 us -> 38.5 us
    all_gather x0 -> x1, waiting for transfers between devices: none -> 171 us  [body(): lax.all_gather(partial_sum.astype(jnp.bfloat16), 'etp')]
    psum x1 -> x0, waiting for transfers between devices: 94.3 us -> none  [body(): lax.psum(partial_sum.astype(jnp.bfloat16), 'etp').astype(jnp.float32)]
    reduce_sum x0 -> x1, other arithmetic: none -> 14.8 us  [body(): jnp.sum(lax.all_gather(partial_sum.astype(jnp.bfloat16), 'etp'), axis=0)]
where the time goes in v1:
time: 839 us; the launch traced here: 832 us
  waiting for transfers between devices  405 us (48%)
  blocking collectives  160 us (19%)
  local copies, waits for them, and re-layouts  146 us (17%)
  starting transfers between devices  38.7 us (5%)
  other arithmetic  38.5 us (5%)
  matrix products  28.6 us (3%)
  between operations  14.8 us (2%)
    all_gather x1, waiting for transfers between devices, body(): lax.all_gather(partial_sum.astype(jnp.bfloat16), 'etp')  171 us
    all_to_all x1, blocking collectives, body(): lax.all_to_all(send_rows, 'expert', split_axis=0, concat_axis=0, tiled=True)  152 us
    all_to_all x1, waiting for transfers between devices, body(): lax.all_to_all(send_grad, 'expert', split_axis=0, concat_axis=0, tiled=True)  118 us
    all_to_all x1, waiting for transfers between devices, body(): lax.all_to_all(totals.astype(jnp.bfloat16), 'expert', split_axis=0, conca...  116 us
    transpose x2, local copies, waits for them, and re-layouts, expert_major(): jnp.transpose(shaped, order)  20.6 us
  transfers between devices with their start and end apart: 5, of which 3 were waited for; matrix products, arithmetic and copies ran while one was open for 13% of the time, Pallas kernels for 0%

profile of v1, /device:TPU:1, one launch (start us, length us, event | category | flops | bytes accessed | tf_op | source)
XLA Modules:
  0.0 831.6 jit_solution(10110135680809178359)
XLA Ops:
  15.4 8.0 gather_fusion
  24.1 13.2 %all-to-all-start = ((bf16[64,1,20]{2,1,0:T(2,128)(2,1)}), bf16[64,1,20]{2,1,0:T(2,128)(2,1)S(1)}, u32[]{:S(2)}, u32[]{:S(2)}) async-start(bf16[64,1,20]{2,1,0:T(2,128)(2,1)} %all_to_all.28), calls=%async_computation | async-start | bytes 65536 | tf_op jit(solution)/shard_map/all_to_all | solution.py:63
  43.5 9.0 %gather.21 = bf16[64,20,2048]{2,1,0:T(8,128)(2,1)} reshape(bf16[1280,2048]{1,0:T(8,128)(2,1)} %gather_fusion.1) | data formatting | bytes 10485760 | tf_op jit(solution)/shard_map/gather | solution.py:57
  58.7 8.9 %gather.23 = bf16[64,20,2048]{2,1,0:T(8,128)(2,1)} reshape(bf16[1280,2048]{1,0:T(8,128)(2,1)} %gather_fusion.2) | data formatting | bytes 10485760 | tf_op jit(solution)/shard_map/gather | solution.py:54
  67.6 10.2 %broadcast_select_fusion = (bf16[64,20,2048]{2,1,0:T(8,128)(2,1)}, bf16[64,20,2048]{2,1,0:T(8,128)(2,1)}) fusion(bf16[64,20,2048]{2,1,0:T(8,128)(2,1)} %gather.23, pred[64,20]{1,0:T(8,128)(4,1)S(1)} %broadcast_in_dim.43, bf16[64,20,2048]{2,1,0:T(8,128)(2,1)} %gather.21), kind=kLoop, calls=%fused_computation.7 | loop fusion | flops 5242880 | bytes 20972800 | tf_op jit(solution)/shard_map/jit(_where)/select_n | solution.py:54
  77.8 151.6 %all_to_all.34 = bf16[64,20,2048]{2,1,0:T(8,128)(2,1)} all-to-all(bf16[64,20,2048]{2,1,0:T(8,128)(2,1)} %get-tuple-element.35), channel_id=1, replica_groups=mesh['expert'=64,'etp'=4] {'expert'}, dimensions={0} | all-to-all | bytes 10485760 | tf_op jit(solution)/shard_map/all_to_all | solution.py:61
  240.2 8.1 copy.98
  248.3 10.3 %copy.99 = bf16[2,64,10,2048]{3,0,2,1:T(2,128)(2,1)} copy(bf16[2,64,10,2048]{3,1,2,0:T(8,128)(2,1)} %bitcast.37) | data formatting | bytes 10485760 | tf_op jit(solution)/shard_map/transpose | solution.py:19
  258.6 117.8 %all-to-all-done.1 = bf16[64,20,2048]{2,1,0:T(8,128)(2,1)} async-done(((bf16[64,20,2048]{2,1,0:T(8,128)(2,1)}), bf16[64,20,2048]{2,1,0:T(8,128)(2,1)}, u32[]{:S(2)}, u32[]{:S(2)}) %all-to-all-start.1) | async-done | bytes 5242912 | tf_op jit(solution)/shard_map/all_to_all | solution.py:62
  376.4 8.5 %copy.95 = bf16[64,20,2048]{2,0,1:T(8,128)(2,1)} copy(bf16[64,20,2048]{2,1,0:T(8,128)(2,1)} %all-to-all-done.1) | data formatting | bytes 10485760 | tf_op jit(solution)/shard_map/all_to_all | solution.py:62
  384.8 10.4 %copy.96 = bf16[2,64,10,2048]{3,0,2,1:T(2,128)(2,1)} copy(bf16[2,64,10,2048]{3,1,2,0:T(8,128)(2,1)} %bitcast.38) | data formatting | bytes 10485760 | tf_op jit(solution)/shard_map/transpose | solution.py:19
  395.2 7.4 fusion.6
  408.5 7.1 convolution_convert_fusion
  415.6 10.2 %copy.102 = bf16[2,640,2048]{2,0,1:T(2,128)(2,1)} copy(bf16[2,640,2048]{2,1,0:T(8,128)(2,1)} %convolution_convert_fusion) | data formatting | bytes 10485760 | tf_op jit(solution)/shard_map/convert_element_type | solution.py:97
  425.8 7.8 copy.103
  434.0 8.5 %psum.7 = bf16[64,1,20]{0,2,1:T(8,128)(2,1)S(1)} all-reduce(bf16[64,1,20]{0,2,1:T(8,128)(2,1)S(1)} %all_to_all.26), channel_id=1, replica_groups=mesh['expert'=64,'etp'=4] {'etp'}, use_global_device_ids=true, to_apply=%region_7.8 | all-reduce | flops 1280 | bytes 5120 | tf_op jit(solution)/shard_map/psum | solution.py:103
  443.3 7.7 all-to-all-start.4
  451.0 171.4 %all-gather.2.cloned.1.call-done = bf16[4,64,20,2048]{3,1,2,0:T(8,128)(2,1)} async-done(((bf16[1,64,20,2048]{3,1,2,0:T(8,128)(2,1)}), bf16[4,64,20,2048]{3,1,2,0:T(8,128)(2,1)}) %all-gather.2.cloned.1.call-update) | async-done | bytes 20971536 | tf_op jit(solution)/shard_map/all_gather | solution.py:100
  622.4 14.8 %reduce_sum.43 = bf16[64,20,2048]{2,0,1:T(8,128)(2,1)} reduce(bf16[4,64,20,2048]{3,1,2,0:T(8,128)(2,1)} %all-gather.2.cloned.1.call-done, bf16[]{:T(256)} %constant.34.clone.1), dimensions={0}, to_apply=%region_4.5 | reduce | flops 7864320 | bytes 26214402 | tf_op jit(solution)/shard_map/reduce_sum | solution.py:100
  637.2 8.1 copy.104
  645.3 11.4 %all-to-all-start.3 = ((bf16[64,20,2048]{2,1,0:T(8,128)(2,1)}), bf16[64,20,2048]{2,1,0:T(8,128)(2,1)}, u32[]{:S(2)}, u32[]{:S(2)}) async-start(bf16[64,20,2048]{2,1,0:T(8,128)(2,1)} %copy.104), calls=%async_computation.3 | async-start | bytes 12582912 | tf_op jit(solution)/shard_map/all_to_all | solution.py:106
  681.8 115.5 %all-to-all-done.3 = bf16[64,20,2048]{2,1,0:T(8,128)(2,1)} async-done(((bf16[64,20,2048]{2,1,0:T(8,128)(2,1)}), bf16[64,20,2048]{2,1,0:T(8,128)(2,1)}, u32[]{:S(2)}, u32[]{:S(2)}) %all-to-all-start.3) | async-done | bytes 5242912 | tf_op jit(solution)/shard_map/all_to_all | solution.py:106
  797.3 9.0 %reshape.137 = bf16[1280,2048]{1,0:T(8,128)(2,1)} reshape(bf16[64,20,2048]{2,1,0:T(8,128)(2,1)} %all-to-all-done.3) | data formatting | bytes 10485760 | tf_op jit(solution)/shard_map/reshape | solution.py:9
  806.3 12.1 %gather_fusion.3 = bf16[1024,2048]{1,0:T(8,128)(2,1)} fusion(bf16[1280,2048]{1,0:T(8,128)(2,1)} %reshape.137, s32[1024]{0:T(1024)S(1)} %broadcast_clamp_fusion), kind=kCustom, calls=%fused_computation.3 | custom fusion | bytes 8392704 | tf_op jit(solution)/shard_map/gather | solution.py:9
  (81 shorter events, 69.9 us)
Async XLA Ops:
  7.2 395.4 %copy-start = (bf16[2,192,2048]{2,1,0:T(8,128)(2,1)S(1)}, bf16[2,192,2048]{2,1,0:T(8,128)(2,1)}, u32[]{:S(2)}) copy-start(bf16[2,192,2048]{2,1,0:T(8,128)(2,1)} %param.13) | copy-start | bytes 4718596
  7.2 30.2 %copy-start.2 = (bf16[128,2048]{1,0:T(8,128)(2,1)S(1)}, bf16[128,2048]{1,0:T(8,128)(2,1)}, u32[]{:S(2)}) copy-start(bf16[128,2048]{1,0:T(8,128)(2,1)} %param.8) | copy-start | bytes 1572868
  24.1 53.7 %all-to-all-start = ((bf16[64,1,20]{2,1,0:T(2,128)(2,1)}), bf16[64,1,20]{2,1,0:T(2,128)(2,1)S(1)}, u32[]{:S(2)}, u32[]{:S(2)}) async-start(bf16[64,1,20]{2,1,0:T(2,128)(2,1)} %all_to_all.28), calls=%async_computation | async-start | bytes 65536 | tf_op jit(solution)/shard_map/all_to_all | solution.py:63
  43.5 9.0 %copy-start.3 = (bf16[128,2048]{1,0:T(8,128)(2,1)S(1)}, bf16[128,2048]{1,0:T(8,128)(2,1)}, u32[]{:S(2)}) copy-start(bf16[128,2048]{1,0:T(8,128)(2,1)} %param.7) | copy-start | bytes 1572868
  229.4 6.4 copy-start.5
  229.4 147.0 %all-to-all-start.1 = ((bf16[64,20,2048]{2,1,0:T(8,128)(2,1)}), bf16[64,20,2048]{2,1,0:T(8,128)(2,1)}, u32[]{:S(2)}, u32[]{:S(2)}) async-start(bf16[64,20,2048]{2,1,0:T(8,128)(2,1)} %get-tuple-element.36), calls=%async_computation.1 | async-start | bytes 12582912 | tf_op jit(solution)/shard_map/all_to_all | solution.py:62
  235.5 386.9 %all-gather.2.cloned.1.call-start = ((), (), s32[]{:S(2)}) async-start(), calls=%async_computation.5 | async-start | bytes 26214400 | tf_op jit(solution)/shard_map/all_gather | solution.py:100
  395.2 7.4 copy-start.4
  407.7 0.8 copy-start.6
  443.3 202.0 %all-to-all-start.4 = ((bf16[64,1,20]{2,1,0:T(2,128)(2,1)}), bf16[64,1,20]{2,1,0:T(2,128)(2,1)S(1)}, u32[]{:S(2)}, u32[]{:S(2)}) async-start(bf16[64,1,20]{2,1,0:T(2,128)(2,1)} %copy.106), calls=%async_computation.4 | async-start | bytes 65536 | tf_op jit(solution)/shard_map/all_to_all | solution.py:109
  645.3 22.5 %slice-start = ((s8[5242880]{0:T(1024)(128)(4,1)}), s8[1048576]{0:T(1024)(128)(4,1)S(1)}, s32[]{:S(2)}) async-start(s8[5242880]{0:T(1024)(128)(4,1)} %bitcast.41), calls=%async_computation.6 | async-start | bytes 2097152
  645.3 152.1 %all-to-all-start.3 = ((bf16[64,20,2048]{2,1,0:T(8,128)(2,1)}), bf16[64,20,2048]{2,1,0:T(8,128)(2,1)}, u32[]{:S(2)}, u32[]{:S(2)}) async-start(bf16[64,20,2048]{2,1,0:T(8,128)(2,1)} %copy.104), calls=%async_computation.3 | async-start | bytes 12582912 | tf_op jit(solution)/shard_map/all_to_all | solution.py:106
  656.9 6.2 copy-start.8
  656.9 10.9 %slice-start.1 = ((s8[5242880]{0:T(1024)(128)(4,1)}), s8[4194304]{0:T(1024)(128)(4,1)S(1)}, s32[]{:S(2)}) async-start(s8[5242880]{0:T(1024)(128)(4,1)} %bitcast.41), calls=%async_computation.7 | async-start | bytes 8388608
  663.1 4.7 copy-start.7
  806.3 18.0 %copy-start.1 = (bf16[2,192,2048]{2,1,0:T(8,128)(2,1)S(1)}, bf16[2,192,2048]{2,1,0:T(8,128)(2,1)}, u32[]{:S(2)}) copy-start(bf16[2,192,2048]{2,1,0:T(8,128)(2,1)} %param.13) | copy-start | bytes 4718596
Sparse Core Ops, SparseCore 0:
  433.8 188.5 all-gather.1
